TPU v7x, 256 devices: a whole 4x4x8 slice. The times are simulated.
256 devices in a mesh: sky: 32 (over y, z_lo, core), loop: 8 (over x, z_hi).
Axes of the slice: x: 4, y: 4, z: 8 (z_hi: 2, z_lo: 4; z = z_hi * 4 + z_lo), core: 2. Of those that a mesh axis runs over, the one named last changes fastest.
Arguments:
- queries: bfloat16 [196608, 256], P(('sky', 'loop')), may hold values from -1 to 1
- keys: bfloat16 [196608, 256], P(('sky', 'loop')), may hold values from -1 to 1
- partner_owner: int32 [196608, 4], P(('sky', 'loop')), may hold values from 0 to 31, as said below
- partner_row: int32 [196608, 4], P(('sky', 'loop')), may hold values from 0 to 767
- partner_count: int32 [196608], P(('sky', 'loop')), may hold values from 1 to 4, as said below
Outputs:
- loss: float32 [196608], P(('sky', 'loop'))
- grad_queries: float32 [196608, 256], P(('sky', 'loop'))
- grad_keys: float32 [196608, 256], P(('sky', 'loop'))
Inputs may be any that keep to these rules, and one draw needn't show every extreme that they name: `partner_owner`: each row names 4 different sky indices, never its own device's sky index; among the rows of one device no index is named more than 192 times, and on every device some index is named exactly 192 times. `partner_count`: some anchor has 4 live partners and some has one.
All inputs are finite; a program needn't handle non-finite values.
Results may differ from a plain program's by a relative error of at most 0.004.
Values may be sent and summed in bfloat16 or wider, within the bound.
A program may use at most 64 MiB of HBM per device.

v0:
```python
import jax
import jax.numpy as jnp
from jax import lax
from jax.sharding import PartitionSpec as P

SCALE = 10.0
EPS = 1e-06


def unit_rows(rows):
    wide = rows.astype(jnp.float32)
    norms = jnp.sqrt(jnp.sum(wide * wide, axis=1, keepdims=True) + EPS)
    return (wide / norms, norms)


def back_unit(unit, norms, grad):
    return (grad - unit * jnp.sum(unit * grad, axis=1, keepdims=True)) / norms


def fold_blocks(carry, pieces, step):
    total_rows = pieces[0].shape[0]
    size = 512
    number = total_rows // size
    split = tuple((piece.reshape((number, size) + piece.shape[1:]) for piece in pieces))
    offsets = size * jnp.arange(number, dtype=jnp.int32)

    def one_turn(summed, item):
        return (step(summed, item[0], item[1]), None)

    result, unused = lax.scan(one_turn, carry, (split, offsets))
    return result


def shards(queries, keys, partner_owner, partner_row, partner_count):
    anchors, width = queries.shape
    slots = partner_owner.shape[1]
    sky_count = lax.axis_size("sky")
    bucket = 2 * anchors * slots // sky_count
    unit_q, norm_q = unit_rows(queries)
    unit_k, norm_k = unit_rows(keys)
    query_rows = unit_q.astype(jnp.bfloat16)
    key_rows = unit_k.astype(jnp.bfloat16)
    mine = lax.axis_index("loop") * anchors + jnp.arange(anchors, dtype=jnp.int32)
    valid = jnp.arange(slots, dtype=jnp.int32)[None, :] < partner_count[:, None]
    inverse = 1.0 / (1.0 + partner_count.astype(jnp.float32))
    flat_owner = partner_owner.reshape(-1)
    owner_hits = (flat_owner[:, None] == jnp.arange(sky_count, dtype=jnp.int32)[None, :]).astype(
        jnp.int32
    )
    earlier = jnp.sum((jnp.cumsum(owner_hits, axis=0) - owner_hits) * owner_hits, axis=1)
    slot_index = flat_owner * bucket + earlier
    requests = (
        jnp.zeros((sky_count * bucket,), jnp.int32).at[slot_index].set(partner_row.reshape(-1))
    )
    incoming = lax.all_to_all(
        requests.reshape(sky_count, bucket), "sky", split_axis=0, concat_axis=0, tiled=True
    )
    wanted = incoming.reshape(-1)
    replies = jnp.take(key_rows, wanted, axis=0)
    answered = lax.all_to_all(
        replies.reshape(sky_count, bucket, width), "sky", split_axis=0, concat_axis=0, tiled=True
    )
    partner_keys = jnp.take(answered.reshape(-1, width), slot_index, axis=0).reshape(
        anchors, slots, width
    )
    outgoing = (
        jnp.zeros((sky_count * bucket, width), jnp.bfloat16)
        .at[slot_index]
        .set(jnp.repeat(query_rows, slots, axis=0))
    )
    partner_logits = SCALE * jnp.einsum(
        "apd,ad->ap", partner_keys, query_rows, preferred_element_type=jnp.float32
    )

    def add_exp(total, block, offset):
        scores = SCALE * jnp.dot(query_rows, block[0].T, preferred_element_type=jnp.float32)
        return total + jnp.sum(jnp.exp(scores), axis=1)

    start_sum = jnp.zeros((anchors,), jnp.float32)
    group_keys = lax.all_gather(key_rows, "loop", axis=0, tiled=True)
    total = fold_blocks(start_sum, (group_keys,), add_exp)
    log_total = jnp.log(total + jnp.sum(jnp.where(valid, jnp.exp(partner_logits), 0.0), axis=1))
    own_logits = SCALE * jnp.sum(
        query_rows.astype(jnp.float32) * key_rows.astype(jnp.float32), axis=1
    )
    loss = log_total - inverse * (
        own_logits + jnp.sum(jnp.where(valid, partner_logits, 0.0), axis=1)
    )
    partner_weights = jnp.where(
        valid, jnp.exp(partner_logits - log_total[:, None]) - inverse[:, None], 0.0
    ).astype(jnp.bfloat16)

    def add_grad(summed, block, offset):
        piece = block[0]
        scores = SCALE * jnp.dot(query_rows, piece.T, preferred_element_type=jnp.float32)
        columns = offset + jnp.arange(piece.shape[0], dtype=jnp.int32)
        target = jnp.where(mine[:, None] == columns[None, :], inverse[:, None], 0.0)
        weights = (jnp.exp(scores - log_total[:, None]) - target).astype(jnp.bfloat16)
        return summed + jnp.dot(weights, piece, preferred_element_type=jnp.float32)

    empty = jnp.zeros((anchors, width), jnp.float32)
    summed_q = fold_blocks(empty, (group_keys,), add_grad)
    grad_unit_q = SCALE * (
        summed_q
        + jnp.einsum(
            "ap,apd->ad", partner_weights, partner_keys, preferred_element_type=jnp.float32
        )
    )
    grad_queries = back_unit(unit_q, norm_q, grad_unit_q)
    all_log_total, all_inverse = (
        lax.all_gather(log_total, "loop", axis=0, tiled=True),
        lax.all_gather(inverse, "loop", axis=0, tiled=True),
    )

    def add_key_grad(summed, block, offset):
        piece = block[0]
        number = piece.shape[0]
        scores = SCALE * jnp.dot(piece, key_rows.T, preferred_element_type=jnp.float32)
        piece_log = lax.dynamic_slice_in_dim(all_log_total, offset, number)
        piece_inverse = lax.dynamic_slice_in_dim(all_inverse, offset, number)
        row_ids = offset + jnp.arange(number, dtype=jnp.int32)
        target = jnp.where(row_ids[:, None] == mine[None, :], piece_inverse[:, None], 0.0)
        weights = (jnp.exp(scores - piece_log[:, None]) - target).astype(jnp.bfloat16)
        return summed + lax.dot_general(
            weights, piece, (((0,), (0,)), ((), ())), preferred_element_type=jnp.float32
        )

    summed_k = fold_blocks(
        empty, (lax.all_gather(query_rows, "loop", axis=0, tiled=True),), add_key_grad
    )
    slot_weights = (
        jnp.zeros((sky_count * bucket,), jnp.bfloat16)
        .at[slot_index]
        .set(partner_weights.reshape(-1))
    )
    got_rows, got_weights = (
        lax.all_to_all(
            outgoing.reshape(sky_count, bucket, width),
            "sky",
            split_axis=0,
            concat_axis=0,
            tiled=True,
        ),
        lax.all_to_all(
            slot_weights.reshape(sky_count, bucket), "sky", split_axis=0, concat_axis=0, tiled=True
        ),
    )
    back_rows = got_rows.reshape(-1, width)
    back_weights = got_weights.reshape(-1)
    partner_grad = jax.ops.segment_sum(
        back_weights.astype(jnp.float32)[:, None] * back_rows.astype(jnp.float32),
        wanted,
        num_segments=anchors,
    )
    grad_keys = back_unit(unit_k, norm_k, SCALE * (summed_k + partner_grad))
    return (loss, grad_queries, grad_keys)


def solution(mesh):
    in_specs = (
        P(("sky", "loop"), None),
        P(("sky", "loop"), None),
        P(("sky", "loop"), None),
        P(("sky", "loop"), None),
        P(("sky", "loop")),
    )
    out_specs = (P(("sky", "loop")), P(("sky", "loop"), None), P(("sky", "loop"), None))
    return jax.shard_map(shards, mesh=mesh, in_specs=in_specs, out_specs=out_specs, check_vma=False)
```

profile of v0, /device:TPU:1, one launch (start us, length us, event | category | flops | bytes accessed | tf_op | source)
XLA Modules:
  0.0 580.1 jit_solution(7854657634066408081)
XLA Ops:
  13.6 9.2 %reduce-window.6 = s32[32,24,128]{2,1,0:T(8,128)S(1)} reduce-window(s32[32,24,128]{2,1,0:T(8,128)S(1)} %fusion.55, s32[]{:T(128)} %constant.48.clone.1), window={size=1x1x128 pad=0_0x0_0x127_0}, to_apply=%region_5.6 | reduce-window | flops 12484608 | bytes 786436 | tf_op jit(solution)/shard_map/reduce-window
  24.8 11.8 %scatter_custom_fusion = s32[6144]{0:T(1024)S(1)} fusion(s32[3072]{0:T(1024)S(1)} %bitcast.109, s32[3072]{0:T(1024)S(1)} %reshape.223, s32[]{:T(128)} %constant.48.clone.1), kind=kCustom, calls=%fused_computation.91 | custom fusion | bytes 24580 | tf_op jit(solution)/shard_map/scatter | solution.py:53
  36.7 17.5 %all_to_all.29 = s32[32,1,192]{2,1,0:T(1,128)S(1)} all-to-all(s32[32,1,192]{2,1,0:T(1,128)S(1)} %all_to_all.18), channel_id=1, replica_groups=mesh['sky'=32,'loop'=8] {'sky'}, dimensions={0} | all-to-all | bytes 49152 | tf_op jit(solution)/shard_map/all_to_all | solution.py:55
  55.5 24.7 %gather_fusion = bf16[6144,256]{1,0:T(8,128)(2,1)S(1)} fusion(bf16[768,256]{1,0:T(8,128)(2,1)S(1)} %copy-done, s32[6144]{0:T(1024)} %broadcast_clamp_fusion), kind=kCustom, calls=%fused_computation | custom fusion | bytes 6316032 | tf_op jit(solution)/shard_map/jit(_take)/gather | solution.py:59
  83.6 4.3 all-to-all-start.1
  95.6 3.5 reshape.239
  99.1 16.1 %scatter_custom_fusion.2 = bf16[6144,256]{1,0:T(8,128)(2,1)} fusion(s32[3072]{0:T(1024)} %bitcast.110, bf16[3072,256]{1,0:T(8,128)(2,1)} %reshape.239, bf16[]{:T(256)} %constant.95.clone.1), kind=kCustom, calls=%fused_computation.50 | custom fusion | bytes 3146240 | tf_op jit(solution)/shard_map/scatter | solution.py:69
  118.6 18.6 %while.33 = (s32[]{:T(128)}, f32[768]{0:T(1024)S(1)}, bf16[12,512,256]{2,1,0:T(8,128)(2,1)}, bf16[768,256]{1,0:T(8,128)(2,1)}, s32[]{:T(128)}, /*index=5*/s32[]{:T(128)}) while((s32[]{:T(128)}, f32[768]{0:T(1024)S(1)}, bf16[12,512,256]{2,1,0:T(8,128)(2,1)}, bf16[768,256]{1,0:T(8,128)(2,1)}, s32[]{:T(128)}, ...), condition=%wide.region_4.5_spmd.clone, body=%wide.region_2.4_spmd.clone.sunk | while | flops 202113792 | bytes 667739 | solution.py:30
  137.2 69.8 %all-to-all-done.1 = bf16[32,192,256]{2,1,0:T(8,128)(2,1)S(1)} async-done(((bf16[32,192,256]{2,1,0:T(8,128)(2,1)}), bf16[32,192,256]{2,1,0:T(8,128)(2,1)S(1)}, u32[]{:S(2)}, u32[]{:S(2)}) %all-to-all-start.1) | async-done | bytes 3145760 | tf_op jit(solution)/shard_map/all_to_all | solution.py:60
  207.1 14.0 %gather_fusion.1 = bf16[3072,256]{1,0:T(8,128)(2,1)} fusion(bf16[6144,256]{1,0:T(8,128)(2,1)S(1)} %bitcast.95, s32[3072]{0:T(1024)} %broadcast_clamp_fusion.1), kind=kCustom, calls=%fused_computation.1 | custom fusion | bytes 3158016 | tf_op jit(solution)/shard_map/jit(_take)/gather | solution.py:63
  223.5 6.5 %fusion.45 = f32[768,1,4]{2,1,0:T(1,128)S(1)} fusion(bf16[768,4,256]{2,1,0:T(4,128)(2,1)S(1)} %gather.15, pred[768,4]{1,0:T(8,128)(4,1)S(1)} %copy-done.12, bf16[768,256,1]{1,0,2:T(8,128)(2,1)S(1)} %bitcast.101), kind=kOutput, calls=%fused_computation.54 | convolution fusion | flops 2359296 | bytes 1981440 | tf_op jit(solution)/shard_map/apd,ad->ap/dot_general | solution.py:71
  231.9 3.7 fusion.44
  235.8 21.7 %scatter_custom_fusion.1 = bf16[6144]{0:T(1024)(128)(2,1)S(1)} fusion(s32[3072]{0:T(1024)} %bitcast.112, bf16[3072]{0:T(1024)(128)(2,1)S(1)} %reshape.231, bf16[]{:T(256)} %constant.95.clone.1), kind=kCustom, calls=%fused_computation.95 | custom fusion | bytes 12800 | tf_op jit(solution)/shard_map/scatter | solution.py:134
  258.2 6.6 %all-to-all-start.2 = ((bf16[32,1,192]{2,1,0:T(2,128)(2,1)}), bf16[32,1,192]{2,1,0:T(2,128)(2,1)S(1)}, u32[]{:S(2)}, u32[]{:S(2)}) async-start(bf16[32,1,192]{2,1,0:T(2,128)(2,1)} %all_to_all.24), calls=%async_computation.2 | async-start | bytes 65536 | tf_op jit(solution)/shard_map/all_to_all | solution.py:144
  264.9 49.0 %while.34 = (s32[]{:T(128)}, f32[768,256]{1,0:T(8,128)S(1)}, bf16[12,512,256]{2,1,0:T(8,128)(2,1)}, bf16[768,256]{1,0:T(8,128)(2,1)S(1)}, f32[768]{0:T(1024)S(1)...) while((s32[]{:T(128)}, f32[768,256]{1,0:T(8,128)S(1)}, ...), condition=%wide.region_13.14_spmd.clone, body=%wide.region_12.13_spmd.clone.sunk | while | flops 405406976 | bytes 2508426 | solution.py:30
  315.5 39.1 %all-gather = f32[8,1,768]{2,1,0:T(1,128)} all-gather(f32[1,1,768]{2,1,0:T(1,128)S(1)} %reshape.252), channel_id=1, replica_groups=mesh['sky'=32,'loop'=8] {'loop'}, dimensions={0}, use_global_device_ids=true | all-gather | bytes 27648 | tf_op jit(solution)/shard_map/all_gather | solution.py:111
  354.6 38.8 %all-gather.1 = f32[8,1,768]{2,1,0:T(1,128)} all-gather(f32[1,1,768]{2,1,0:T(1,128)S(1)} %reshape.254), channel_id=1, replica_groups=mesh['sky'=32,'loop'=8] {'loop'}, dimensions={0}, use_global_device_ids=true | all-gather | bytes 27648 | tf_op jit(solution)/shard_map/all_gather | solution.py:112
  394.1 20.4 %all-to-all-start.3 = ((bf16[32,192,256]{2,1,0:T(8,128)(2,1)}), bf16[32,192,256]{2,1,0:T(8,128)(2,1)S(1)}, u32[]{:S(2)}, u32[]{:S(2)}) async-start(bf16[32,192,256]{2,1,0:T(8,128)(2,1)} %bitcast.17), calls=%async_computation.3 | async-start | bytes 6291456 | tf_op jit(solution)/shard_map/all_to_all | solution.py:137
  414.5 112.3 %while.35 = (s32[]{:T(128)}, f32[768,256]{1,0:T(8,128)}, bf16[12,512,256]{2,1,0:T(8,128)(2,1)}, bf16[768,256]{1,0:T(8,128)(2,1)S(1)}, s32[12]{0:T(128)}, /*index...) while((s32[]{:T(128)}, f32[768,256]{1,0:T(8,128)}, ...), condition=%wide.region_16.17_spmd.clone, body=%wide.region_15.16_spmd.clone.sunk | while | flops 405406976 | bytes 2514620 | solution.py:30
  420.8 2.9 fusion.90
  429.9 3.2 fusion.90
  439.3 3.2 fusion.90
  448.7 3.2 fusion.90
  458.1 3.2 fusion.90
  467.4 3.2 fusion.90
  476.8 3.2 fusion.90
  486.2 3.2 fusion.90
  495.6 3.2 fusion.90
  505.0 3.2 fusion.90
  514.3 3.2 fusion.90
  523.7 3.2 fusion.90
  528.4 42.2 %scatter_custom_fusion.3 = f32[768,256]{1,0:T(8,128)} fusion(f32[768,256]{1,0:T(8,128)} %get-tuple-element.111, s32[6144]{0:T(1024)} %reshape.245, bf16[6144,256]{1,0:T(8,128)(2,1)S(1)} %bitcast.97, f32[6144]{0:T(1024)} %reshape.201), kind=kCustom, calls=%fused_computation.47 | custom fusion | flops 4718592 | bytes 3956736 | tf_op jit(solution)/shard_map/scatter-add | solution.py:150
  (230 shorter events, 152.2 us)
Async XLA Ops:
  7.2 5.3 copy-start.11
  7.2 111.4 %all-gather.5.cloned.1.call-start = ((), (), s32[]{:S(2)}) async-start(), calls=%async_computation.4 | async-start | bytes 3538944 | tf_op jit(solution)/shard_map/all_gather | solution.py:80
  9.6 2.9 copy-start.13
  13.1 10.3 %copy-start.18 = (s32[768,4]{0,1:T(4,128)S(1)}, s32[768,4]{0,1:T(4,128)}, u32[]{:S(2)}) copy-start(s32[768,4]{0,1:T(4,128)} %param.14) | copy-start | bytes 36868
  23.0 32.5 %copy-start = (bf16[768,256]{1,0:T(8,128)(2,1)S(1)}, bf16[768,256]{1,0:T(8,128)(2,1)}, u32[]{:S(2)}) copy-start(bf16[768,256]{1,0:T(8,128)(2,1)} %get-tuple-element.411) | copy-start | bytes 1179652
  24.2 0.6 copy-start.16
  54.2 0.6 copy-start.9
  54.3 0.6 copy-start.8
  83.6 123.5 %all-to-all-start.1 = ((bf16[32,192,256]{2,1,0:T(8,128)(2,1)}), bf16[32,192,256]{2,1,0:T(8,128)(2,1)S(1)}, u32[]{:S(2)}, u32[]{:S(2)}) async-start(bf16[32,192,256]{2,1,0:T(8,128)(2,1)} %broadcast_select_fusion), calls=%async_computation.1 | async-start | bytes 6291456 | tf_op jit(solution)/shard_map/all_to_all | solution.py:60
  87.9 326.7 %all-gather.7.cloned.1.call-start = ((), (), s32[]{:S(2)}) async-start(), calls=%async_computation.5 | async-start | bytes 3538944 | tf_op jit(solution)/shard_map/all_gather | solution.py:129
  221.0 2.4 copy-start.3
  221.0 2.4 copy-start.12
  223.4 6.6 %copy-start.6 = (bf16[768,4,256]{2,1,0:T(4,128)(2,1)}, bf16[768,4,256]{2,1,0:T(4,128)(2,1)S(1)}, u32[]{:S(2)}) copy-start(bf16[768,4,256]{2,1,0:T(4,128)(2,1)S(1)} %gather.15) | copy-start | bytes 4718596
  223.5 6.6 %copy-start.15 = (s32[768]{0:T(1024)S(1)}, s32[768]{0:T(1024)}, u32[]{:S(2)}) copy-start(s32[768]{0:T(1024)} %param.15) | copy-start | bytes 9220
  223.5 7.0 %copy-start.17 = (f32[768]{0:T(1024)S(1)}, f32[768]{0:T(1024)}, u32[]{:S(2)}) copy-start(f32[768]{0:T(1024)} %get-tuple-element.231) | copy-start | bytes 9220
  230.1 1.8 copy-start.7
  231.9 33.0 %copy-start.5 = (f32[768,256]{1,0:T(8,128)S(1)}, f32[768,256]{1,0:T(8,128)}, u32[]{:S(2)}) copy-start(f32[768,256]{1,0:T(8,128)} %custom-call.1) | copy-start | bytes 2359300
  258.2 135.2 %all-to-all-start.2 = ((bf16[32,1,192]{2,1,0:T(2,128)(2,1)}), bf16[32,1,192]{2,1,0:T(2,128)(2,1)S(1)}, u32[]{:S(2)}, u32[]{:S(2)}) async-start(bf16[32,1,192]{2,1,0:T(2,128)(2,1)} %all_to_all.24), calls=%async_computation.2 | async-start | bytes 65536 | tf_op jit(solution)/shard_map/all_to_all | solution.py:144
  264.9 49.0 %copy-start.2 = (bf16[768,256]{1,0:T(8,128)(2,1)S(1)}, bf16[768,256]{1,0:T(8,128)(2,1)}, u32[]{:S(2)}) copy-start(bf16[768,256]{1,0:T(8,128)(2,1)} %param.11) | copy-start | bytes 1179652
  264.9 49.0 %copy-start.14 = (f32[768]{0:T(1024)S(1)}, f32[768]{0:T(1024)}, u32[]{:S(2)}) copy-start(f32[768]{0:T(1024)} %copy-done.13) | copy-start | bytes 9220
  393.4 0.6 copy-start.10
  394.1 134.3 %all-to-all-start.3 = ((bf16[32,192,256]{2,1,0:T(8,128)(2,1)}), bf16[32,192,256]{2,1,0:T(8,128)(2,1)S(1)}, u32[]{:S(2)}, u32[]{:S(2)}) async-start(bf16[32,192,256]{2,1,0:T(8,128)(2,1)} %bitcast.17), calls=%async_computation.3 | async-start | bytes 6291456 | tf_op jit(solution)/shard_map/all_to_all | solution.py:137
  528.4 42.2 %copy-start.1 = (bf16[768,256]{1,0:T(8,128)(2,1)S(1)}, bf16[768,256]{1,0:T(8,128)(2,1)}, u32[]{:S(2)}) copy-start(bf16[768,256]{1,0:T(8,128)(2,1)} %param.12) | copy-start | bytes 1179652
  570.6 1.6 copy-start.4
Sparse Core Ops, SparseCore 0:
  12.6 90.2 all-gather.4
  105.5 85.9 all-gather.6
where the time goes:
time: 584 us; the launch traced here: 580 us
  local copies, waits for them, and re-layouts  164 us (28%)
  blocking collectives  95.4 us (16%)
  matrix products  91.6 us (16%)
  other arithmetic  86.9 us (15%)
  waiting for transfers between devices  70.6 us (12%)
  starting transfers between devices  31.4 us (5%)
  loops' own time  25.9 us (4%)
  between operations  14.5 us (2%)
    all_to_all x1, waiting for transfers between devices, shards(): lax.all_to_all(replies.reshape(sky_count, bucket, width), 'sky', split_ax...  69.8 us
    scatter-add x1, other arithmetic, shards(): jax.ops.segment_sum(back_weights.astype(jnp.float32)[:, None] * back_rows...  42.2 us
    all_gather x1, blocking collectives, shards(): lax.all_gather(log_total, 'loop', axis=0, tiled=True)  39.1 us
    all_gather x1, blocking collectives, shards(): lax.all_gather(inverse, 'loop', axis=0, tiled=True)  38.8 us
    dot_general x12, matrix products, add_key_grad(): lax.dot_general(weights, piece, (((0,), (0,)), ((), ())), preferred_eleme...  37.6 us
    dynamic_slice x24, local copies, waits for them, and re-layouts, fold_blocks(): result, unused = lax.scan(one_turn, carry, (split, offsets))  30.9 us
    another operation x3, loops' own time, fold_blocks(): result, unused = lax.scan(one_turn, carry, (split, offsets))  25.9 us
    dot_general x12, matrix products, add_grad(): return summed + jnp.dot(weights, piece, preferred_element_type=jnp.float32)  25.6 us
  transfers between devices with their start and end apart: 5, of which 1 were waited for; matrix products, arithmetic and copies ran while one was open for 50% of the time, Pallas kernels for 0%

commit v1 on v0

--- a/solution.py
+++ b/solution.py
@@ -109,7 +109,9 @@
     grad_queries = back_unit(unit_q, norm_q, grad_unit_q)
     all_log_total, all_inverse = (
         lax.all_gather(log_total, "loop", axis=0, tiled=True),
-        lax.all_gather(inverse, "loop", axis=0, tiled=True),
+        jnp.concatenate(
+            lax.all_to_all(jnp.stack([inverse] * lax.axis_size("loop")), "loop", 0, 0), axis=0
+        ),
     )
 
     def add_key_grad(summed, block, offset):

time: 584 us -> 548 us (0.938)
  blocking collectives: 95.4 us -> 56.9 us
    all_gather x1 -> x0, blocking collectives: 38.8 us -> none  [shards(): lax.all_gather(inverse, 'loop', axis=0, tiled=True)]
    all_to_all x1, starting transfers between devices: 20.4 us -> 14 us  [shards(): lax.all_to_all(outgoing.reshape(sky_count, bucket, width), 'sky', split_a...]
    all_to_all x0 -> x1, starting transfers between devices: none -> 6.13 us  [shards(): lax.all_to_all(jnp.stack([inverse] * lax.axis_size('loop')), 'loop', 0, 0)]
  transfers between devices with their start and end apart: 5 -> 6, of which waited for: 1 -> 1; matrix products, arithmetic and copies ran while one was open for 50% -> 54% of each run, Pallas kernels for 0% -> 0%
where the time goes in v1:
time: 548 us; the launch traced here: 543 us
  local copies, waits for them, and re-layouts  165 us (30%)
  matrix products  91.6 us (17%)
  other arithmetic  87.5 us (16%)
  waiting for transfers between devices  70.6 us (13%)
  blocking collectives  56.9 us (10%)
  starting transfers between devices  31.1 us (6%)
  loops' own time  25.9 us (5%)
  between operations  14.5 us (3%)
    all_to_all x1, waiting for transfers between devices, shards(): lax.all_to_all(replies.reshape(sky_count, bucket, width), 'sky', split_ax...  69.8 us
    scatter-add x1, other arithmetic, shards(): jax.ops.segment_sum(back_weights.astype(jnp.float32)[:, None] * back_rows...  42.2 us
    all_gather x1, blocking collectives, shards(): lax.all_gather(log_total, 'loop', axis=0, tiled=True)  39.4 us
    dot_general x12, matrix products, add_key_grad(): lax.dot_general(weights, piece, (((0,), (0,)), ((), ())), preferred_eleme...  37.6 us
    dynamic_slice x24, local copies, waits for them, and re-layouts, fold_blocks(): result, unused = lax.scan(one_turn, carry, (split, offsets))  30.9 us
    another operation x3, loops' own time, fold_blocks(): result, unused = lax.scan(one_turn, carry, (split, offsets))  25.9 us
    dot_general x12, matrix products, add_grad(): return summed + jnp.dot(weights, piece, preferred_element_type=jnp.float32)  25.6 us
    gather x1, local copies, waits for them, and re-layouts, shards(): replies = jnp.take(key_rows, wanted, axis=0)  24.7 us
  transfers between devices with their start and end apart: 6, of which 1 were waited for; matrix products, arithmetic and copies ran while one was open for 54% of the time, Pallas kernels for 0%

profile of v1, /device:TPU:1, one launch (start us, length us, event | category | flops | bytes accessed | tf_op | source)
XLA Modules:
  0.0 543.3 jit_solution(7137594246318376062)
XLA Ops:
  13.6 9.2 %reduce-window.6 = s32[32,24,128]{2,1,0:T(8,128)S(1)} reduce-window(s32[32,24,128]{2,1,0:T(8,128)S(1)} %fusion.55, s32[]{:T(128)} %constant.48.clone.1), window={size=1x1x128 pad=0_0x0_0x127_0}, to_apply=%region_5.6 | reduce-window | flops 12484608 | bytes 786436 | tf_op jit(solution)/shard_map/reduce-window
  24.8 11.8 %scatter_custom_fusion = s32[6144]{0:T(1024)S(1)} fusion(s32[3072]{0:T(1024)S(1)} %bitcast.109, s32[3072]{0:T(1024)S(1)} %reshape.235, s32[]{:T(128)} %constant.48.clone.1), kind=kCustom, calls=%fused_computation.91 | custom fusion | bytes 24580 | tf_op jit(solution)/shard_map/scatter | solution.py:53
  36.7 17.5 %all_to_all.35 = s32[32,1,192]{2,1,0:T(1,128)S(1)} all-to-all(s32[32,1,192]{2,1,0:T(1,128)S(1)} %all_to_all.22), channel_id=1, replica_groups=mesh['sky'=32,'loop'=8] {'sky'}, dimensions={0} | all-to-all | bytes 49152 | tf_op jit(solution)/shard_map/all_to_all | solution.py:55
  55.5 24.7 %gather_fusion = bf16[6144,256]{1,0:T(8,128)(2,1)S(1)} fusion(bf16[768,256]{1,0:T(8,128)(2,1)S(1)} %copy-done, s32[6144]{0:T(1024)} %broadcast_clamp_fusion), kind=kCustom, calls=%fused_computation | custom fusion | bytes 6316032 | tf_op jit(solution)/shard_map/jit(_take)/gather | solution.py:59
  83.6 4.3 all-to-all-start.1
  95.6 3.5 reshape.251
  99.1 16.1 %scatter_custom_fusion.2 = bf16[6144,256]{1,0:T(8,128)(2,1)} fusion(s32[3072]{0:T(1024)} %bitcast.110, bf16[3072,256]{1,0:T(8,128)(2,1)} %reshape.251, bf16[]{:T(256)} %constant.95.clone.1), kind=kCustom, calls=%fused_computation.50 | custom fusion | bytes 3146240 | tf_op jit(solution)/shard_map/scatter | solution.py:69
  118.6 18.6 %while.33 = (s32[]{:T(128)}, f32[768]{0:T(1024)S(1)}, bf16[12,512,256]{2,1,0:T(8,128)(2,1)}, bf16[768,256]{1,0:T(8,128)(2,1)}, s32[]{:T(128)}, /*index=5*/s32[]{:T(128)}) while((s32[]{:T(128)}, f32[768]{0:T(1024)S(1)}, bf16[12,512,256]{2,1,0:T(8,128)(2,1)}, bf16[768,256]{1,0:T(8,128)(2,1)}, s32[]{:T(128)}, ...), condition=%wide.region_4.5_spmd.clone, body=%wide.region_2.4_spmd.clone.sunk | while | flops 202113792 | bytes 667739 | solution.py:30
  137.2 69.8 %all-to-all-done.1 = bf16[32,192,256]{2,1,0:T(8,128)(2,1)S(1)} async-done(((bf16[32,192,256]{2,1,0:T(8,128)(2,1)}), bf16[32,192,256]{2,1,0:T(8,128)(2,1)S(1)}, u32[]{:S(2)}, u32[]{:S(2)}) %all-to-all-start.1) | async-done | bytes 3145760 | tf_op jit(solution)/shard_map/all_to_all | solution.py:60
  207.1 14.0 %gather_fusion.1 = bf16[3072,256]{1,0:T(8,128)(2,1)} fusion(bf16[6144,256]{1,0:T(8,128)(2,1)S(1)} %bitcast.95, s32[3072]{0:T(1024)} %broadcast_clamp_fusion.1), kind=kCustom, calls=%fused_computation.1 | custom fusion | bytes 3158016 | tf_op jit(solution)/shard_map/jit(_take)/gather | solution.py:63
  223.5 6.5 %fusion.45 = f32[768,1,4]{2,1,0:T(1,128)S(1)} fusion(bf16[768,4,256]{2,1,0:T(4,128)(2,1)S(1)} %gather.15, pred[768,4]{1,0:T(8,128)(4,1)S(1)} %copy-done.12, bf16[768,256,1]{1,0,2:T(8,128)(2,1)S(1)} %bitcast.101), kind=kOutput, calls=%fused_computation.54 | convolution fusion | flops 2359296 | bytes 1981440 | tf_op jit(solution)/shard_map/apd,ad->ap/dot_general | solution.py:71
  231.9 3.7 fusion.44
  235.8 21.7 %scatter_custom_fusion.1 = bf16[6144]{0:T(1024)(128)(2,1)S(1)} fusion(s32[3072]{0:T(1024)} %bitcast.112, bf16[3072]{0:T(1024)(128)(2,1)S(1)} %reshape.243, bf16[]{:T(256)} %constant.95.clone.1), kind=kCustom, calls=%fused_computation.95 | custom fusion | bytes 12800 | tf_op jit(solution)/shard_map/scatter | solution.py:136
  258.2 6.6 %all-to-all-start.3 = ((bf16[32,1,192]{2,1,0:T(2,128)(2,1)}), bf16[32,1,192]{2,1,0:T(2,128)(2,1)S(1)}, u32[]{:S(2)}, u32[]{:S(2)}) async-start(bf16[32,1,192]{2,1,0:T(2,128)(2,1)} %all_to_all.29), calls=%async_computation.3 | async-start | bytes 65536 | tf_op jit(solution)/shard_map/all_to_all | solution.py:146
  264.9 49.0 %while.34 = (s32[]{:T(128)}, f32[768,256]{1,0:T(8,128)S(1)}, bf16[12,512,256]{2,1,0:T(8,128)(2,1)}, bf16[768,256]{1,0:T(8,128)(2,1)S(1)}, f32[768]{0:T(1024)S(1)...) while((s32[]{:T(128)}, f32[768,256]{1,0:T(8,128)S(1)}, ...), condition=%wide.region_13.14_spmd.clone, body=%wide.region_12.13_spmd.clone.sunk | while | flops 405406976 | bytes 2508426 | solution.py:30
  315.0 6.1 %all-to-all-start.2 = ((f32[8,1,768]{2,1,0:T(1,128)}), f32[8,1,768]{2,1,0:T(1,128)S(1)}, u32[]{:S(2)}, u32[]{:S(2)}) async-start(f32[8,1,768]{2,1,0:T(1,128)} %stack.2), calls=%async_computation.2 | async-start | bytes 49152 | tf_op jit(solution)/shard_map/all_to_all | solution.py:113
  322.3 39.4 %all-gather = f32[8,1,768]{2,1,0:T(1,128)} all-gather(f32[1,1,768]{2,1,0:T(1,128)S(1)} %reshape.264), channel_id=1, replica_groups=mesh['sky'=32,'loop'=8] {'loop'}, dimensions={0}, use_global_device_ids=true | all-gather | bytes 27648 | tf_op jit(solution)/shard_map/all_gather | solution.py:111
  362.3 14.0 %all-to-all-start.4 = ((bf16[32,192,256]{2,1,0:T(8,128)(2,1)}), bf16[32,192,256]{2,1,0:T(8,128)(2,1)S(1)}, u32[]{:S(2)}, u32[]{:S(2)}) async-start(bf16[32,192,256]{2,1,0:T(8,128)(2,1)} %bitcast.17), calls=%async_computation.4 | async-start | bytes 6291456 | tf_op jit(solution)/shard_map/all_to_all | solution.py:139
  379.2 112.3 %while.35 = (s32[]{:T(128)}, f32[768,256]{1,0:T(8,128)}, bf16[12,512,256]{2,1,0:T(8,128)(2,1)}, bf16[768,256]{1,0:T(8,128)(2,1)S(1)}, s32[12]{0:T(128)}, /*index...) while((s32[]{:T(128)}, f32[768,256]{1,0:T(8,128)}, ...), condition=%wide.region_16.17_spmd.clone, body=%wide.region_15.16_spmd.clone.sunk | while | flops 405406976 | bytes 2514620 | solution.py:30
  385.5 2.9 fusion.90
  394.6 3.2 fusion.90
  404.0 3.2 fusion.90
  413.4 3.2 fusion.90
  422.7 3.2 fusion.90
  432.1 3.2 fusion.90
  441.5 3.2 fusion.90
  450.9 3.2 fusion.90
  460.3 3.2 fusion.90
  469.7 3.2 fusion.90
  479.0 3.2 fusion.90
  488.4 3.2 fusion.90
  491.5 42.2 %scatter_custom_fusion.3 = f32[768,256]{1,0:T(8,128)} fusion(f32[768,256]{1,0:T(8,128)} %get-tuple-element.111, s32[6144]{0:T(1024)} %reshape.257, bf16[6144,256]{1,0:T(8,128)(2,1)S(1)} %bitcast.97, f32[6144]{0:T(1024)} %reshape.213), kind=kCustom, calls=%fused_computation.47 | custom fusion | flops 4718592 | bytes 3956736 | tf_op jit(solution)/shard_map/scatter-add | solution.py:152
  (233 shorter events, 154.2 us)
Async XLA Ops:
  7.2 5.3 copy-start.11
  7.2 111.4 %all-gather.4.cloned.1.call-start = ((), (), s32[]{:S(2)}) async-start(), calls=%async_computation.5 | async-start | bytes 3538944 | tf_op jit(solution)/shard_map/all_gather | solution.py:80
  9.6 2.9 copy-start.13
  13.1 10.3 %copy-start.19 = (s32[768,4]{0,1:T(4,128)S(1)}, s32[768,4]{0,1:T(4,128)}, u32[]{:S(2)}) copy-start(s32[768,4]{0,1:T(4,128)} %param.14) | copy-start | bytes 36868
  23.0 32.5 %copy-start = (bf16[768,256]{1,0:T(8,128)(2,1)S(1)}, bf16[768,256]{1,0:T(8,128)(2,1)}, u32[]{:S(2)}) copy-start(bf16[768,256]{1,0:T(8,128)(2,1)} %get-tuple-element.411) | copy-start | bytes 1179652
  24.2 0.6 copy-start.17
  54.2 0.6 copy-start.9
  54.3 0.6 copy-start.8
  83.6 123.5 %all-to-all-start.1 = ((bf16[32,192,256]{2,1,0:T(8,128)(2,1)}), bf16[32,192,256]{2,1,0:T(8,128)(2,1)S(1)}, u32[]{:S(2)}, u32[]{:S(2)}) async-start(bf16[32,192,256]{2,1,0:T(8,128)(2,1)} %broadcast_select_fusion), calls=%async_computation.1 | async-start | bytes 6291456 | tf_op jit(solution)/shard_map/all_to_all | solution.py:60
  87.9 291.4 %all-gather.6.cloned.1.call-start = ((), (), s32[]{:S(2)}) async-start(), calls=%async_computation.6 | async-start | bytes 3538944 | tf_op jit(solution)/shard_map/all_gather | solution.py:131
  221.0 2.4 copy-start.3
  221.0 2.4 copy-start.12
  223.4 6.6 %copy-start.6 = (bf16[768,4,256]{2,1,0:T(4,128)(2,1)}, bf16[768,4,256]{2,1,0:T(4,128)(2,1)S(1)}, u32[]{:S(2)}) copy-start(bf16[768,4,256]{2,1,0:T(4,128)(2,1)S(1)} %gather.15) | copy-start | bytes 4718596
  223.5 6.6 %copy-start.15 = (s32[768]{0:T(1024)S(1)}, s32[768]{0:T(1024)}, u32[]{:S(2)}) copy-start(s32[768]{0:T(1024)} %param.15) | copy-start | bytes 9220
  223.5 7.0 %copy-start.18 = (f32[768]{0:T(1024)S(1)}, f32[768]{0:T(1024)}, u32[]{:S(2)}) copy-start(f32[768]{0:T(1024)} %get-tuple-element.231) | copy-start | bytes 9220
  230.1 1.8 copy-start.7
  231.9 33.0 %copy-start.5 = (f32[768,256]{1,0:T(8,128)S(1)}, f32[768,256]{1,0:T(8,128)}, u32[]{:S(2)}) copy-start(f32[768,256]{1,0:T(8,128)} %custom-call.1) | copy-start | bytes 2359300
  258.2 56.1 %all-to-all-start.3 = ((bf16[32,1,192]{2,1,0:T(2,128)(2,1)}), bf16[32,1,192]{2,1,0:T(2,128)(2,1)S(1)}, u32[]{:S(2)}, u32[]{:S(2)}) async-start(bf16[32,1,192]{2,1,0:T(2,128)(2,1)} %all_to_all.29), calls=%async_computation.3 | async-start | bytes 65536 | tf_op jit(solution)/shard_map/all_to_all | solution.py:146
  264.9 49.0 %copy-start.2 = (bf16[768,256]{1,0:T(8,128)(2,1)S(1)}, bf16[768,256]{1,0:T(8,128)(2,1)}, u32[]{:S(2)}) copy-start(bf16[768,256]{1,0:T(8,128)(2,1)} %param.11) | copy-start | bytes 1179652
  264.9 49.0 %copy-start.14 = (f32[768]{0:T(1024)S(1)}, f32[768]{0:T(1024)}, u32[]{:S(2)}) copy-start(f32[768]{0:T(1024)} %copy-done.13) | copy-start | bytes 9220
  314.4 47.3 %copy-start.10 = (bf16[32,1,192]{2,1,0:T(2,128)(2,1)}, bf16[32,1,192]{2,1,0:T(2,128)(2,1)S(1)}, u32[]{:S(2)}) copy-start(bf16[32,1,192]{2,1,0:T(2,128)(2,1)S(1)} %all-to-all-done.3) | copy-start | bytes 36868
  315.0 46.7 %all-to-all-start.2 = ((f32[8,1,768]{2,1,0:T(1,128)}), f32[8,1,768]{2,1,0:T(1,128)S(1)}, u32[]{:S(2)}, u32[]{:S(2)}) async-start(f32[8,1,768]{2,1,0:T(1,128)} %stack.2), calls=%async_computation.2 | async-start | bytes 49152 | tf_op jit(solution)/shard_map/all_to_all | solution.py:113
  361.7 0.6 copy-start.16
  362.3 129.3 %all-to-all-start.4 = ((bf16[32,192,256]{2,1,0:T(8,128)(2,1)}), bf16[32,192,256]{2,1,0:T(8,128)(2,1)S(1)}, u32[]{:S(2)}, u32[]{:S(2)}) async-start(bf16[32,192,256]{2,1,0:T(8,128)(2,1)} %bitcast.17), calls=%async_computation.4 | async-start | bytes 6291456 | tf_op jit(solution)/shard_map/all_to_all | solution.py:139
  491.5 42.2 %copy-start.1 = (bf16[768,256]{1,0:T(8,128)(2,1)S(1)}, bf16[768,256]{1,0:T(8,128)(2,1)}, u32[]{:S(2)}) copy-start(bf16[768,256]{1,0:T(8,128)(2,1)} %param.12) | copy-start | bytes 1179652
  533.7 1.6 copy-start.4
Sparse Core Ops, SparseCore 0:
  12.6 90.2 all-gather.3
  105.5 85.9 all-gather.5
